TPU v7x, 128 devices: a whole 4x4x4 slice. The times are simulated.
128 devices in a mesh: ctx: 32 (over y, z_lo, x), page: 4 (over z_hi, core).
Axes of the slice: x: 4, y: 4, z: 4 (z_hi: 2, z_lo: 2; z = z_hi * 2 + z_lo), core: 2. Of those that a mesh axis runs over, the one named last changes fastest.
Arguments:
- queries: bfloat16 [8192, 8192], P('ctx', 'page'), may hold values from -200 to 200
- keys: bfloat16 [8192, 512], P('ctx', 'page'), may hold values from -6 to 6
- values: bfloat16 [8192, 512], P('ctx', 'page'), may hold values from -6 to 6
- span_table: int32 [64], replicated, may hold values from 0 to 63, each once
- page_slots: int32 [64], replicated, may hold values from 0 to 63, each once
Outputs:
- attended: bfloat16 [8192, 8192], P('ctx', 'page')
- cache_pages: bfloat16 [64, 4, 2, 128, 128], P('ctx')
- cache_scales: float32 [64, 4, 2], P('ctx')
Inputs may be any that keep to these rules, and one draw needn't show every extreme that they name: Stored span i (rows i * 128 to (i + 1) * 128 - 1) holds prompt positions span_table[i] * 128 onward; every value appears once. `page_slots`: every slot is named by exactly one page.
All inputs are finite; a program needn't handle non-finite values. Where the computation divides by a largest or mean magnitude, that divisor is 1e-20 or more.
Results may differ from a plain program's by a relative error of at most 0.0055.
Values may be sent and summed in bfloat16 or wider, within the bound.
No kernel may reach another device: no remote copies, remote signals or barrier semaphores. Data moves between devices by JAX's collectives and lax.ppermute only.
A program may use at most 64 MiB of HBM per device.

v0:
```python
import math
import jax
import jax.numpy as jnp
from jax import lax
from jax.sharding import PartitionSpec as P

DH = 128
PAGE = 128
SPAN = 128


def side_by_side(arrays, axis, dim, along):
    both = jnp.concatenate(arrays, axis=along)
    result, at, gathered = (lax.all_gather(both, axis, axis=dim, tiled=True), 0, [])
    for a in arrays:
        gathered.append(lax.slice_in_dim(result, at, at + a.shape[along], axis=along))
        at += a.shape[along]
    return tuple(gathered)


def on_device(queries, keys, values, span_table, page_slots):
    rows = queries.shape[0]
    kv_here = keys.shape[1] // DH
    q_here = queries.shape[1] // DH
    group = q_here // kv_here
    ctx_index = lax.axis_index("ctx")
    table_size = span_table.shape[0]
    scale = DH ** (-0.5)

    def token_positions(start, count):
        span_ids = start // SPAN + jnp.arange(count // SPAN, dtype=jnp.int32)
        onehot = span_ids[:, None] == jnp.arange(table_size, dtype=jnp.int32)[None, :]
        placed = jnp.sum(jnp.where(onehot, span_table[None, :], 0), axis=1)
        inner = jnp.arange(SPAN, dtype=jnp.int32)
        return (placed[:, None] * SPAN + inner[None, :]).reshape(count)

    query_pos = token_positions(ctx_index * rows, rows)
    query_heads = queries.reshape(rows, kv_here, group, DH)
    slots_here = rows // PAGE
    first_slot = ctx_index * slots_here
    page_ids = jnp.arange(page_slots.shape[0], dtype=jnp.int32)
    wanted = [
        jnp.sum(jnp.where(page_slots == first_slot + j, page_ids, 0)) for j in range(slots_here)
    ]

    def collect(held, piece):
        count = piece.shape[0]
        updated = []
        for j in range(slots_here):
            offset = wanted[j] * PAGE
            inside = (offset >= 0) & (offset + PAGE <= count)
            clamped = jnp.clip(offset, 0, count - PAGE)
            picked = lax.dynamic_slice_in_dim(piece, clamped, PAGE, 0)
            updated.append(jnp.where(inside, picked, held[j]))
        return jnp.stack(updated, axis=0)

    start_state = (
        jnp.full((kv_here, group, rows), -1e30, jnp.float32),
        jnp.zeros((kv_here, group, rows), jnp.float32),
        jnp.zeros((kv_here, group, rows, DH), jnp.float32),
    )
    empty_pages = jnp.zeros((slots_here, PAGE, kv_here * DH), jnp.bfloat16)
    state = start_state
    key_pages = empty_pages
    value_pages = empty_pages
    key_piece, value_piece = side_by_side((keys, values), "ctx", 0, 1)
    count = key_piece.shape[0]
    key_pos = token_positions(jnp.int32(0), count)
    attend_state = state
    attend_key_piece = key_piece.reshape(count, kv_here, DH)
    attend_value_piece = value_piece.reshape(count, kv_here, DH)
    attend_count = attend_key_piece.shape[0]
    width = math.gcd(attend_count, 512)
    blocks = attend_count // width
    key_blocks = attend_key_piece.reshape(blocks, width, kv_here, DH)
    value_blocks = attend_value_piece.reshape(blocks, width, kv_here, DH)
    pos_blocks = key_pos.reshape(blocks, width)

    def step(carry, block):
        top, total, summed = carry
        key_block, value_block, pos_block = block
        score = (
            jnp.einsum("qhgd,khd->hgqk", query_heads, key_block, preferred_element_type=jnp.float32)
            * scale
        )
        keep = pos_block[None, :] <= query_pos[:, None]
        score = jnp.where(keep[None, None], score, -1e30)
        new_top = jnp.maximum(top, jnp.max(score, axis=-1))
        factor = jnp.exp(top - new_top)
        weight = jnp.where(keep[None, None], jnp.exp(score - new_top[..., None]), 0.0)
        total = total * factor + jnp.sum(weight, axis=-1)
        update = jnp.einsum(
            "hgqk,khd->hgqd",
            weight.astype(jnp.bfloat16),
            value_block,
            preferred_element_type=jnp.float32,
        )
        summed = summed * factor[..., None] + update
        return ((new_top, total, summed), None)

    attend_state, unused = lax.scan(step, attend_state, (key_blocks, value_blocks, pos_blocks))
    state = attend_state
    state, key_pages, value_pages = (
        state,
        collect(key_pages, key_piece),
        collect(value_pages, value_piece),
    )
    key_pages = key_pages.reshape(slots_here, PAGE, kv_here, DH).transpose(0, 2, 1, 3)
    value_pages = value_pages.reshape(slots_here, PAGE, kv_here, DH).transpose(0, 2, 1, 3)
    local_raw = jnp.stack([key_pages, value_pages], axis=2)
    raw = lax.all_gather(local_raw, "page", axis=1, tiled=True)
    top, total, summed = state
    result = summed / total[..., None]
    attended = jnp.transpose(result, (2, 0, 1, 3)).reshape(rows, q_here * DH).astype(jnp.bfloat16)
    raw_float = raw.astype(jnp.float32)
    cache_scales = jnp.max(jnp.abs(raw_float), axis=(3, 4)) + 1e-06
    cache_pages = (raw_float / cache_scales[..., None, None]).astype(jnp.bfloat16)
    return (attended, cache_pages, cache_scales)


def solution(mesh):
    placed = (P("ctx", "page"), P("ctx", "page"), P("ctx", "page"), P(), P())
    return jax.shard_map(
        on_device,
        mesh=mesh,
        in_specs=placed,
        out_specs=(P("ctx", "page"), P("ctx", None, None, None, None), P("ctx", None, None)),
        check_vma=False,
    )
```

profile of v0, /device:TPU:1, one launch (start us, length us, event | category | flops | bytes accessed | tf_op | source)
XLA Modules:
  0.0 446.5 jit_solution(1242300555539706280)
XLA Ops:
  7.2 1.5 pad_maximum_fusion
  8.8 1.3 fusion.27
  12.3 1.5 copy.31
  14.8 135.6 %all-gather.2.cloned.1.call-done = bf16[8192,256]{1,0:T(8,128)(2,1)} async-done(((bf16[256,256]{1,0:T(8,128)(2,1)}), bf16[8192,256]{1,0:T(8,128)(2,1)}) %all-gather.2.cloned.1.call-update) | async-done | bytes 4194320 | tf_op jit(solution)/shard_map/all_gather | solution.py:14
  150.4 2.5 fusion.29
  153.0 1.3 copy-done.1
  154.3 29.1 %all_gather.7 = bf16[2,4,2,128,128]{4,3,2,1,0:T(8,128)(2,1)S(1)} all-gather(bf16[2,1,2,128,128]{4,3,2,1,0:T(8,128)(2,1)S(1)} %pad_maximum_fusion.1), channel_id=1, replica_groups=mesh['ctx'=32,'page'=4] {'page'}, dimensions={1}, use_global_device_ids=true | all-gather | bytes 655360 | tf_op jit(solution)/shard_map/all_gather | solution.py:111
  185.4 250.4 %while.15 = (s32[]{:T(128)}, f32[1,16,256]{2,1,0:T(8,128)S(1)}, f32[1,16,256]{2,1,0:T(8,128)S(1)}, f32[1,16,256,128]{3,2,1,0:T(8,128)}, s32[16,512]{1,0:T(8,128)...) while((s32[]{:T(128)}, f32[1,16,256]{2,1,0:T(8,128)S(1)}, ...), condition=%wide.region_5.6_spmd.clone, body=%wide.region_2.5_spmd.clone.sunk | while | flops 1102733568 | bytes 65020080 | solution.py:101
  185.6 4.6 %fusion.37 = (f32[16,256]{1,0:T(8,128)S(1)}, f32[512,256,16]{1,0,2:T(8,128)}) fusion(pred[256,512]{0,1:T(8,128)(4,1)S(1)} %broadcast_compare_fusion.2, bf16[256,1,16,128]{3,0,2,1:T(8,128)(2,1)S(1)} %get-tuple-element.251, bf16[16,512,1,128]{3,1,2,0:T(8,128)(2,1)S(1)} %get-tuple-element.250, s32[]{:T(128)S(6)} %copy.48), kind=kOutput, calls=%fused_computation.3.clone.1 | convolution fusion | flops 543158272 | bytes 9715716 | tf_op jit(solution)/shard_map/while/body/eval_jaxpr/qhgd,khd->hgqk/dot_general | solution.py:83
  190.2 4.6 %fusion.39 = f32[16,256]{1,0:T(8,128)S(1)} fusion(f32[512,256,16]{1,0,2:T(8,128)} %get-tuple-element.221, f32[16,256]{1,0:T(8,128)S(1)} %bitcast.113, pred[256,512]{0,1:T(8,128)(4,1)S(1)} %broadcast_compare_fusion.2), kind=kLoop, calls=%fused_computation.5.clone.1 | loop fusion | flops 10481664 | bytes 8552448 | tf_op jit(solution)/shard_map/while/body/eval_jaxpr/reduce_sum | solution.py:91
  194.8 1.2 copy-done
  196.0 4.7 %bitcast_add_fusion.6 = f32[1,16,256,128]{3,2,1,0:T(8,128)} fusion(f32[1,16,256,128]{3,2,1,0:T(8,128)} %get-tuple-element.237, f32[512,256,16]{1,0,2:T(8,128)S(1)} %copy-done, f32[16,256]{1,0:T(8,128)S(1)} %bitcast.114, pred[256,512]{0,1:T(8,128)(4,1)S(1)} %broadcast_compare_fusion.2, f32[16,256]{1,0:T(8,128)S(1)} %get-tuple-element.222, ...), kind=kOutput, calls=%fused_computation.9.clone.1 | convolution fusion | flops 548929536 | bytes 12877829 | tf_op jit(solution)/shard_map/while/body/eval_jaxpr/hgqk,khd->hgqd/dot_general | solution.py:92
  201.0 4.6 %fusion.37 = (f32[16,256]{1,0:T(8,128)S(1)}, f32[512,256,16]{1,0,2:T(8,128)}) fusion(pred[256,512]{0,1:T(8,128)(4,1)S(1)} %broadcast_compare_fusion.2, bf16[256,1,16,128]{3,0,2,1:T(8,128)(2,1)S(1)} %get-tuple-element.251, bf16[16,512,1,128]{3,1,2,0:T(8,128)(2,1)S(1)} %get-tuple-element.250, s32[]{:T(128)S(6)} %copy.48), kind=kOutput, calls=%fused_computation.3.clone.1 | convolution fusion | flops 543158272 | bytes 9715716 | tf_op jit(solution)/shard_map/while/body/eval_jaxpr/qhgd,khd->hgqk/dot_general | solution.py:83
  205.6 4.6 %fusion.39 = f32[16,256]{1,0:T(8,128)S(1)} fusion(f32[512,256,16]{1,0,2:T(8,128)} %get-tuple-element.221, f32[16,256]{1,0:T(8,128)S(1)} %bitcast.113, pred[256,512]{0,1:T(8,128)(4,1)S(1)} %broadcast_compare_fusion.2), kind=kLoop, calls=%fused_computation.5.clone.1 | loop fusion | flops 10481664 | bytes 8552448 | tf_op jit(solution)/shard_map/while/body/eval_jaxpr/reduce_sum | solution.py:91
  210.2 1.2 copy-done
  211.4 5.0 %bitcast_add_fusion.6 = f32[1,16,256,128]{3,2,1,0:T(8,128)} fusion(f32[1,16,256,128]{3,2,1,0:T(8,128)} %get-tuple-element.237, f32[512,256,16]{1,0,2:T(8,128)S(1)} %copy-done, f32[16,256]{1,0:T(8,128)S(1)} %bitcast.114, pred[256,512]{0,1:T(8,128)(4,1)S(1)} %broadcast_compare_fusion.2, f32[16,256]{1,0:T(8,128)S(1)} %get-tuple-element.222, ...), kind=kOutput, calls=%fused_computation.9.clone.1 | convolution fusion | flops 548929536 | bytes 12877829 | tf_op jit(solution)/shard_map/while/body/eval_jaxpr/hgqk,khd->hgqd/dot_general | solution.py:92
  216.6 4.6 %fusion.37 = (f32[16,256]{1,0:T(8,128)S(1)}, f32[512,256,16]{1,0,2:T(8,128)}) fusion(pred[256,512]{0,1:T(8,128)(4,1)S(1)} %broadcast_compare_fusion.2, bf16[256,1,16,128]{3,0,2,1:T(8,128)(2,1)S(1)} %get-tuple-element.251, bf16[16,512,1,128]{3,1,2,0:T(8,128)(2,1)S(1)} %get-tuple-element.250, s32[]{:T(128)S(6)} %copy.48), kind=kOutput, calls=%fused_computation.3.clone.1 | convolution fusion | flops 543158272 | bytes 9715716 | tf_op jit(solution)/shard_map/while/body/eval_jaxpr/qhgd,khd->hgqk/dot_general | solution.py:83
  221.2 4.6 %fusion.39 = f32[16,256]{1,0:T(8,128)S(1)} fusion(f32[512,256,16]{1,0,2:T(8,128)} %get-tuple-element.221, f32[16,256]{1,0:T(8,128)S(1)} %bitcast.113, pred[256,512]{0,1:T(8,128)(4,1)S(1)} %broadcast_compare_fusion.2), kind=kLoop, calls=%fused_computation.5.clone.1 | loop fusion | flops 10481664 | bytes 8552448 | tf_op jit(solution)/shard_map/while/body/eval_jaxpr/reduce_sum | solution.py:91
  225.9 1.2 copy-done
  227.1 5.0 %bitcast_add_fusion.6 = f32[1,16,256,128]{3,2,1,0:T(8,128)} fusion(f32[1,16,256,128]{3,2,1,0:T(8,128)} %get-tuple-element.237, f32[512,256,16]{1,0,2:T(8,128)S(1)} %copy-done, f32[16,256]{1,0:T(8,128)S(1)} %bitcast.114, pred[256,512]{0,1:T(8,128)(4,1)S(1)} %broadcast_compare_fusion.2, f32[16,256]{1,0:T(8,128)S(1)} %get-tuple-element.222, ...), kind=kOutput, calls=%fused_computation.9.clone.1 | convolution fusion | flops 548929536 | bytes 12877829 | tf_op jit(solution)/shard_map/while/body/eval_jaxpr/hgqk,khd->hgqd/dot_general | solution.py:92
  232.3 4.6 %fusion.37 = (f32[16,256]{1,0:T(8,128)S(1)}, f32[512,256,16]{1,0,2:T(8,128)}) fusion(pred[256,512]{0,1:T(8,128)(4,1)S(1)} %broadcast_compare_fusion.2, bf16[256,1,16,128]{3,0,2,1:T(8,128)(2,1)S(1)} %get-tuple-element.251, bf16[16,512,1,128]{3,1,2,0:T(8,128)(2,1)S(1)} %get-tuple-element.250, s32[]{:T(128)S(6)} %copy.48), kind=kOutput, calls=%fused_computation.3.clone.1 | convolution fusion | flops 543158272 | bytes 9715716 | tf_op jit(solution)/shard_map/while/body/eval_jaxpr/qhgd,khd->hgqk/dot_general | solution.py:83
  236.9 4.6 %fusion.39 = f32[16,256]{1,0:T(8,128)S(1)} fusion(f32[512,256,16]{1,0,2:T(8,128)} %get-tuple-element.221, f32[16,256]{1,0:T(8,128)S(1)} %bitcast.113, pred[256,512]{0,1:T(8,128)(4,1)S(1)} %broadcast_compare_fusion.2), kind=kLoop, calls=%fused_computation.5.clone.1 | loop fusion | flops 10481664 | bytes 8552448 | tf_op jit(solution)/shard_map/while/body/eval_jaxpr/reduce_sum | solution.py:91
  241.5 1.2 copy-done
  242.7 5.0 %bitcast_add_fusion.6 = f32[1,16,256,128]{3,2,1,0:T(8,128)} fusion(f32[1,16,256,128]{3,2,1,0:T(8,128)} %get-tuple-element.237, f32[512,256,16]{1,0,2:T(8,128)S(1)} %copy-done, f32[16,256]{1,0:T(8,128)S(1)} %bitcast.114, pred[256,512]{0,1:T(8,128)(4,1)S(1)} %broadcast_compare_fusion.2, f32[16,256]{1,0:T(8,128)S(1)} %get-tuple-element.222, ...), kind=kOutput, calls=%fused_computation.9.clone.1 | convolution fusion | flops 548929536 | bytes 12877829 | tf_op jit(solution)/shard_map/while/body/eval_jaxpr/hgqk,khd->hgqd/dot_general | solution.py:92
  248.0 4.6 %fusion.37 = (f32[16,256]{1,0:T(8,128)S(1)}, f32[512,256,16]{1,0,2:T(8,128)}) fusion(pred[256,512]{0,1:T(8,128)(4,1)S(1)} %broadcast_compare_fusion.2, bf16[256,1,16,128]{3,0,2,1:T(8,128)(2,1)S(1)} %get-tuple-element.251, bf16[16,512,1,128]{3,1,2,0:T(8,128)(2,1)S(1)} %get-tuple-element.250, s32[]{:T(128)S(6)} %copy.48), kind=kOutput, calls=%fused_computation.3.clone.1 | convolution fusion | flops 543158272 | bytes 9715716 | tf_op jit(solution)/shard_map/while/body/eval_jaxpr/qhgd,khd->hgqk/dot_general | solution.py:83
  252.6 4.6 %fusion.39 = f32[16,256]{1,0:T(8,128)S(1)} fusion(f32[512,256,16]{1,0,2:T(8,128)} %get-tuple-element.221, f32[16,256]{1,0:T(8,128)S(1)} %bitcast.113, pred[256,512]{0,1:T(8,128)(4,1)S(1)} %broadcast_compare_fusion.2), kind=kLoop, calls=%fused_computation.5.clone.1 | loop fusion | flops 10481664 | bytes 8552448 | tf_op jit(solution)/shard_map/while/body/eval_jaxpr/reduce_sum | solution.py:91
  257.2 1.2 copy-done
  258.4 5.0 %bitcast_add_fusion.6 = f32[1,16,256,128]{3,2,1,0:T(8,128)} fusion(f32[1,16,256,128]{3,2,1,0:T(8,128)} %get-tuple-element.237, f32[512,256,16]{1,0,2:T(8,128)S(1)} %copy-done, f32[16,256]{1,0:T(8,128)S(1)} %bitcast.114, pred[256,512]{0,1:T(8,128)(4,1)S(1)} %broadcast_compare_fusion.2, f32[16,256]{1,0:T(8,128)S(1)} %get-tuple-element.222, ...), kind=kOutput, calls=%fused_computation.9.clone.1 | convolution fusion | flops 548929536 | bytes 12877829 | tf_op jit(solution)/shard_map/while/body/eval_jaxpr/hgqk,khd->hgqd/dot_general | solution.py:92
  263.6 4.6 %fusion.37 = (f32[16,256]{1,0:T(8,128)S(1)}, f32[512,256,16]{1,0,2:T(8,128)}) fusion(pred[256,512]{0,1:T(8,128)(4,1)S(1)} %broadcast_compare_fusion.2, bf16[256,1,16,128]{3,0,2,1:T(8,128)(2,1)S(1)} %get-tuple-element.251, bf16[16,512,1,128]{3,1,2,0:T(8,128)(2,1)S(1)} %get-tuple-element.250, s32[]{:T(128)S(6)} %copy.48), kind=kOutput, calls=%fused_computation.3.clone.1 | convolution fusion | flops 543158272 | bytes 9715716 | tf_op jit(solution)/shard_map/while/body/eval_jaxpr/qhgd,khd->hgqk/dot_general | solution.py:83
  268.2 4.6 %fusion.39 = f32[16,256]{1,0:T(8,128)S(1)} fusion(f32[512,256,16]{1,0,2:T(8,128)} %get-tuple-element.221, f32[16,256]{1,0:T(8,128)S(1)} %bitcast.113, pred[256,512]{0,1:T(8,128)(4,1)S(1)} %broadcast_compare_fusion.2), kind=kLoop, calls=%fused_computation.5.clone.1 | loop fusion | flops 10481664 | bytes 8552448 | tf_op jit(solution)/shard_map/while/body/eval_jaxpr/reduce_sum | solution.py:91
  272.9 1.2 copy-done
  274.1 5.0 %bitcast_add_fusion.6 = f32[1,16,256,128]{3,2,1,0:T(8,128)} fusion(f32[1,16,256,128]{3,2,1,0:T(8,128)} %get-tuple-element.237, f32[512,256,16]{1,0,2:T(8,128)S(1)} %copy-done, f32[16,256]{1,0:T(8,128)S(1)} %bitcast.114, pred[256,512]{0,1:T(8,128)(4,1)S(1)} %broadcast_compare_fusion.2, f32[16,256]{1,0:T(8,128)S(1)} %get-tuple-element.222, ...), kind=kOutput, calls=%fused_computation.9.clone.1 | convolution fusion | flops 548929536 | bytes 12877829 | tf_op jit(solution)/shard_map/while/body/eval_jaxpr/hgqk,khd->hgqd/dot_general | solution.py:92
  279.3 4.6 %fusion.37 = (f32[16,256]{1,0:T(8,128)S(1)}, f32[512,256,16]{1,0,2:T(8,128)}) fusion(pred[256,512]{0,1:T(8,128)(4,1)S(1)} %broadcast_compare_fusion.2, bf16[256,1,16,128]{3,0,2,1:T(8,128)(2,1)S(1)} %get-tuple-element.251, bf16[16,512,1,128]{3,1,2,0:T(8,128)(2,1)S(1)} %get-tuple-element.250, s32[]{:T(128)S(6)} %copy.48), kind=kOutput, calls=%fused_computation.3.clone.1 | convolution fusion | flops 543158272 | bytes 9715716 | tf_op jit(solution)/shard_map/while/body/eval_jaxpr/qhgd,khd->hgqk/dot_general | solution.py:83
  283.9 4.6 %fusion.39 = f32[16,256]{1,0:T(8,128)S(1)} fusion(f32[512,256,16]{1,0,2:T(8,128)} %get-tuple-element.221, f32[16,256]{1,0:T(8,128)S(1)} %bitcast.113, pred[256,512]{0,1:T(8,128)(4,1)S(1)} %broadcast_compare_fusion.2), kind=kLoop, calls=%fused_computation.5.clone.1 | loop fusion | flops 10481664 | bytes 8552448 | tf_op jit(solution)/shard_map/while/body/eval_jaxpr/reduce_sum | solution.py:91
  289.7 5.0 %bitcast_add_fusion.6 = f32[1,16,256,128]{3,2,1,0:T(8,128)} fusion(f32[1,16,256,128]{3,2,1,0:T(8,128)} %get-tuple-element.237, f32[512,256,16]{1,0,2:T(8,128)S(1)} %copy-done, f32[16,256]{1,0:T(8,128)S(1)} %bitcast.114, pred[256,512]{0,1:T(8,128)(4,1)S(1)} %broadcast_compare_fusion.2, f32[16,256]{1,0:T(8,128)S(1)} %get-tuple-element.222, ...), kind=kOutput, calls=%fused_computation.9.clone.1 | convolution fusion | flops 548929536 | bytes 12877829 | tf_op jit(solution)/shard_map/while/body/eval_jaxpr/hgqk,khd->hgqd/dot_general | solution.py:92
  295.0 4.6 %fusion.37 = (f32[16,256]{1,0:T(8,128)S(1)}, f32[512,256,16]{1,0,2:T(8,128)}) fusion(pred[256,512]{0,1:T(8,128)(4,1)S(1)} %broadcast_compare_fusion.2, bf16[256,1,16,128]{3,0,2,1:T(8,128)(2,1)S(1)} %get-tuple-element.251, bf16[16,512,1,128]{3,1,2,0:T(8,128)(2,1)S(1)} %get-tuple-element.250, s32[]{:T(128)S(6)} %copy.48), kind=kOutput, calls=%fused_computation.3.clone.1 | convolution fusion | flops 543158272 | bytes 9715716 | tf_op jit(solution)/shard_map/while/body/eval_jaxpr/qhgd,khd->hgqk/dot_general | solution.py:83
  299.6 4.6 %fusion.39 = f32[16,256]{1,0:T(8,128)S(1)} fusion(f32[512,256,16]{1,0,2:T(8,128)} %get-tuple-element.221, f32[16,256]{1,0:T(8,128)S(1)} %bitcast.113, pred[256,512]{0,1:T(8,128)(4,1)S(1)} %broadcast_compare_fusion.2), kind=kLoop, calls=%fused_computation.5.clone.1 | loop fusion | flops 10481664 | bytes 8552448 | tf_op jit(solution)/shard_map/while/body/eval_jaxpr/reduce_sum | solution.py:91
  305.4 5.0 %bitcast_add_fusion.6 = f32[1,16,256,128]{3,2,1,0:T(8,128)} fusion(f32[1,16,256,128]{3,2,1,0:T(8,128)} %get-tuple-element.237, f32[512,256,16]{1,0,2:T(8,128)S(1)} %copy-done, f32[16,256]{1,0:T(8,128)S(1)} %bitcast.114, pred[256,512]{0,1:T(8,128)(4,1)S(1)} %broadcast_compare_fusion.2, f32[16,256]{1,0:T(8,128)S(1)} %get-tuple-element.222, ...), kind=kOutput, calls=%fused_computation.9.clone.1 | convolution fusion | flops 548929536 | bytes 12877829 | tf_op jit(solution)/shard_map/while/body/eval_jaxpr/hgqk,khd->hgqd/dot_general | solution.py:92
  310.7 4.6 %fusion.37 = (f32[16,256]{1,0:T(8,128)S(1)}, f32[512,256,16]{1,0,2:T(8,128)}) fusion(pred[256,512]{0,1:T(8,128)(4,1)S(1)} %broadcast_compare_fusion.2, bf16[256,1,16,128]{3,0,2,1:T(8,128)(2,1)S(1)} %get-tuple-element.251, bf16[16,512,1,128]{3,1,2,0:T(8,128)(2,1)S(1)} %get-tuple-element.250, s32[]{:T(128)S(6)} %copy.48), kind=kOutput, calls=%fused_computation.3.clone.1 | convolution fusion | flops 543158272 | bytes 9715716 | tf_op jit(solution)/shard_map/while/body/eval_jaxpr/qhgd,khd->hgqk/dot_general | solution.py:83
  315.3 4.6 %fusion.39 = f32[16,256]{1,0:T(8,128)S(1)} fusion(f32[512,256,16]{1,0,2:T(8,128)} %get-tuple-element.221, f32[16,256]{1,0:T(8,128)S(1)} %bitcast.113, pred[256,512]{0,1:T(8,128)(4,1)S(1)} %broadcast_compare_fusion.2), kind=kLoop, calls=%fused_computation.5.clone.1 | loop fusion | flops 10481664 | bytes 8552448 | tf_op jit(solution)/shard_map/while/body/eval_jaxpr/reduce_sum | solution.py:91
  321.1 5.0 %bitcast_add_fusion.6 = f32[1,16,256,128]{3,2,1,0:T(8,128)} fusion(f32[1,16,256,128]{3,2,1,0:T(8,128)} %get-tuple-element.237, f32[512,256,16]{1,0,2:T(8,128)S(1)} %copy-done, f32[16,256]{1,0:T(8,128)S(1)} %bitcast.114, pred[256,512]{0,1:T(8,128)(4,1)S(1)} %broadcast_compare_fusion.2, f32[16,256]{1,0:T(8,128)S(1)} %get-tuple-element.222, ...), kind=kOutput, calls=%fused_computation.9.clone.1 | convolution fusion | flops 548929536 | bytes 12877829 | tf_op jit(solution)/shard_map/while/body/eval_jaxpr/hgqk,khd->hgqd/dot_general | solution.py:92
  326.3 4.6 %fusion.37 = (f32[16,256]{1,0:T(8,128)S(1)}, f32[512,256,16]{1,0,2:T(8,128)}) fusion(pred[256,512]{0,1:T(8,128)(4,1)S(1)} %broadcast_compare_fusion.2, bf16[256,1,16,128]{3,0,2,1:T(8,128)(2,1)S(1)} %get-tuple-element.251, bf16[16,512,1,128]{3,1,2,0:T(8,128)(2,1)S(1)} %get-tuple-element.250, s32[]{:T(128)S(6)} %copy.48), kind=kOutput, calls=%fused_computation.3.clone.1 | convolution fusion | flops 543158272 | bytes 9715716 | tf_op jit(solution)/shard_map/while/body/eval_jaxpr/qhgd,khd->hgqk/dot_general | solution.py:83
  330.9 4.6 %fusion.39 = f32[16,256]{1,0:T(8,128)S(1)} fusion(f32[512,256,16]{1,0,2:T(8,128)} %get-tuple-element.221, f32[16,256]{1,0:T(8,128)S(1)} %bitcast.113, pred[256,512]{0,1:T(8,128)(4,1)S(1)} %broadcast_compare_fusion.2), kind=kLoop, calls=%fused_computation.5.clone.1 | loop fusion | flops 10481664 | bytes 8552448 | tf_op jit(solution)/shard_map/while/body/eval_jaxpr/reduce_sum | solution.py:91
  336.8 5.0 %bitcast_add_fusion.6 = f32[1,16,256,128]{3,2,1,0:T(8,128)} fusion(f32[1,16,256,128]{3,2,1,0:T(8,128)} %get-tuple-element.237, f32[512,256,16]{1,0,2:T(8,128)S(1)} %copy-done, f32[16,256]{1,0:T(8,128)S(1)} %bitcast.114, pred[256,512]{0,1:T(8,128)(4,1)S(1)} %broadcast_compare_fusion.2, f32[16,256]{1,0:T(8,128)S(1)} %get-tuple-element.222, ...), kind=kOutput, calls=%fused_computation.9.clone.1 | convolution fusion | flops 548929536 | bytes 12877829 | tf_op jit(solution)/shard_map/while/body/eval_jaxpr/hgqk,khd->hgqd/dot_general | solution.py:92
  342.0 4.6 %fusion.37 = (f32[16,256]{1,0:T(8,128)S(1)}, f32[512,256,16]{1,0,2:T(8,128)}) fusion(pred[256,512]{0,1:T(8,128)(4,1)S(1)} %broadcast_compare_fusion.2, bf16[256,1,16,128]{3,0,2,1:T(8,128)(2,1)S(1)} %get-tuple-element.251, bf16[16,512,1,128]{3,1,2,0:T(8,128)(2,1)S(1)} %get-tuple-element.250, s32[]{:T(128)S(6)} %copy.48), kind=kOutput, calls=%fused_computation.3.clone.1 | convolution fusion | flops 543158272 | bytes 9715716 | tf_op jit(solution)/shard_map/while/body/eval_jaxpr/qhgd,khd->hgqk/dot_general | solution.py:83
  346.6 4.6 %fusion.39 = f32[16,256]{1,0:T(8,128)S(1)} fusion(f32[512,256,16]{1,0,2:T(8,128)} %get-tuple-element.221, f32[16,256]{1,0:T(8,128)S(1)} %bitcast.113, pred[256,512]{0,1:T(8,128)(4,1)S(1)} %broadcast_compare_fusion.2), kind=kLoop, calls=%fused_computation.5.clone.1 | loop fusion | flops 10481664 | bytes 8552448 | tf_op jit(solution)/shard_map/while/body/eval_jaxpr/reduce_sum | solution.py:91
  352.4 5.0 %bitcast_add_fusion.6 = f32[1,16,256,128]{3,2,1,0:T(8,128)} fusion(f32[1,16,256,128]{3,2,1,0:T(8,128)} %get-tuple-element.237, f32[512,256,16]{1,0,2:T(8,128)S(1)} %copy-done, f32[16,256]{1,0:T(8,128)S(1)} %bitcast.114, pred[256,512]{0,1:T(8,128)(4,1)S(1)} %broadcast_compare_fusion.2, f32[16,256]{1,0:T(8,128)S(1)} %get-tuple-element.222, ...), kind=kOutput, calls=%fused_computation.9.clone.1 | convolution fusion | flops 548929536 | bytes 12877829 | tf_op jit(solution)/shard_map/while/body/eval_jaxpr/hgqk,khd->hgqd/dot_general | solution.py:92
  357.7 4.6 %fusion.37 = (f32[16,256]{1,0:T(8,128)S(1)}, f32[512,256,16]{1,0,2:T(8,128)}) fusion(pred[256,512]{0,1:T(8,128)(4,1)S(1)} %broadcast_compare_fusion.2, bf16[256,1,16,128]{3,0,2,1:T(8,128)(2,1)S(1)} %get-tuple-element.251, bf16[16,512,1,128]{3,1,2,0:T(8,128)(2,1)S(1)} %get-tuple-element.250, s32[]{:T(128)S(6)} %copy.48), kind=kOutput, calls=%fused_computation.3.clone.1 | convolution fusion | flops 543158272 | bytes 9715716 | tf_op jit(solution)/shard_map/while/body/eval_jaxpr/qhgd,khd->hgqk/dot_general | solution.py:83
  362.3 4.6 %fusion.39 = f32[16,256]{1,0:T(8,128)S(1)} fusion(f32[512,256,16]{1,0,2:T(8,128)} %get-tuple-element.221, f32[16,256]{1,0:T(8,128)S(1)} %bitcast.113, pred[256,512]{0,1:T(8,128)(4,1)S(1)} %broadcast_compare_fusion.2), kind=kLoop, calls=%fused_computation.5.clone.1 | loop fusion | flops 10481664 | bytes 8552448 | tf_op jit(solution)/shard_map/while/body/eval_jaxpr/reduce_sum | solution.py:91
  368.1 5.0 %bitcast_add_fusion.6 = f32[1,16,256,128]{3,2,1,0:T(8,128)} fusion(f32[1,16,256,128]{3,2,1,0:T(8,128)} %get-tuple-element.237, f32[512,256,16]{1,0,2:T(8,128)S(1)} %copy-done, f32[16,256]{1,0:T(8,128)S(1)} %bitcast.114, pred[256,512]{0,1:T(8,128)(4,1)S(1)} %broadcast_compare_fusion.2, f32[16,256]{1,0:T(8,128)S(1)} %get-tuple-element.222, ...), kind=kOutput, calls=%fused_computation.9.clone.1 | convolution fusion | flops 548929536 | bytes 12877829 | tf_op jit(solution)/shard_map/while/body/eval_jaxpr/hgqk,khd->hgqd/dot_general | solution.py:92
  373.3 4.6 %fusion.37 = (f32[16,256]{1,0:T(8,128)S(1)}, f32[512,256,16]{1,0,2:T(8,128)}) fusion(pred[256,512]{0,1:T(8,128)(4,1)S(1)} %broadcast_compare_fusion.2, bf16[256,1,16,128]{3,0,2,1:T(8,128)(2,1)S(1)} %get-tuple-element.251, bf16[16,512,1,128]{3,1,2,0:T(8,128)(2,1)S(1)} %get-tuple-element.250, s32[]{:T(128)S(6)} %copy.48), kind=kOutput, calls=%fused_computation.3.clone.1 | convolution fusion | flops 543158272 | bytes 9715716 | tf_op jit(solution)/shard_map/while/body/eval_jaxpr/qhgd,khd->hgqk/dot_general | solution.py:83
  377.9 4.6 %fusion.39 = f32[16,256]{1,0:T(8,128)S(1)} fusion(f32[512,256,16]{1,0,2:T(8,128)} %get-tuple-element.221, f32[16,256]{1,0:T(8,128)S(1)} %bitcast.113, pred[256,512]{0,1:T(8,128)(4,1)S(1)} %broadcast_compare_fusion.2), kind=kLoop, calls=%fused_computation.5.clone.1 | loop fusion | flops 10481664 | bytes 8552448 | tf_op jit(solution)/shard_map/while/body/eval_jaxpr/reduce_sum | solution.py:91
  383.8 5.0 %bitcast_add_fusion.6 = f32[1,16,256,128]{3,2,1,0:T(8,128)} fusion(f32[1,16,256,128]{3,2,1,0:T(8,128)} %get-tuple-element.237, f32[512,256,16]{1,0,2:T(8,128)S(1)} %copy-done, f32[16,256]{1,0:T(8,128)S(1)} %bitcast.114, pred[256,512]{0,1:T(8,128)(4,1)S(1)} %broadcast_compare_fusion.2, f32[16,256]{1,0:T(8,128)S(1)} %get-tuple-element.222, ...), kind=kOutput, calls=%fused_computation.9.clone.1 | convolution fusion | flops 548929536 | bytes 12877829 | tf_op jit(solution)/shard_map/while/body/eval_jaxpr/hgqk,khd->hgqd/dot_general | solution.py:92
  389.0 4.6 %fusion.37 = (f32[16,256]{1,0:T(8,128)S(1)}, f32[512,256,16]{1,0,2:T(8,128)}) fusion(pred[256,512]{0,1:T(8,128)(4,1)S(1)} %broadcast_compare_fusion.2, bf16[256,1,16,128]{3,0,2,1:T(8,128)(2,1)S(1)} %get-tuple-element.251, bf16[16,512,1,128]{3,1,2,0:T(8,128)(2,1)S(1)} %get-tuple-element.250, s32[]{:T(128)S(6)} %copy.48), kind=kOutput, calls=%fused_computation.3.clone.1 | convolution fusion | flops 543158272 | bytes 9715716 | tf_op jit(solution)/shard_map/while/body/eval_jaxpr/qhgd,khd->hgqk/dot_general | solution.py:83
  393.6 4.6 %fusion.39 = f32[16,256]{1,0:T(8,128)S(1)} fusion(f32[512,256,16]{1,0,2:T(8,128)} %get-tuple-element.221, f32[16,256]{1,0:T(8,128)S(1)} %bitcast.113, pred[256,512]{0,1:T(8,128)(4,1)S(1)} %broadcast_compare_fusion.2), kind=kLoop, calls=%fused_computation.5.clone.1 | loop fusion | flops 10481664 | bytes 8552448 | tf_op jit(solution)/shard_map/while/body/eval_jaxpr/reduce_sum | solution.py:91
  399.4 5.0 %bitcast_add_fusion.6 = f32[1,16,256,128]{3,2,1,0:T(8,128)} fusion(f32[1,16,256,128]{3,2,1,0:T(8,128)} %get-tuple-element.237, f32[512,256,16]{1,0,2:T(8,128)S(1)} %copy-done, f32[16,256]{1,0:T(8,128)S(1)} %bitcast.114, pred[256,512]{0,1:T(8,128)(4,1)S(1)} %broadcast_compare_fusion.2, f32[16,256]{1,0:T(8,128)S(1)} %get-tuple-element.222, ...), kind=kOutput, calls=%fused_computation.9.clone.1 | convolution fusion | flops 548929536 | bytes 12877829 | tf_op jit(solution)/shard_map/while/body/eval_jaxpr/hgqk,khd->hgqd/dot_general | solution.py:92
  404.7 4.6 %fusion.37 = (f32[16,256]{1,0:T(8,128)S(1)}, f32[512,256,16]{1,0,2:T(8,128)}) fusion(pred[256,512]{0,1:T(8,128)(4,1)S(1)} %broadcast_compare_fusion.2, bf16[256,1,16,128]{3,0,2,1:T(8,128)(2,1)S(1)} %get-tuple-element.251, bf16[16,512,1,128]{3,1,2,0:T(8,128)(2,1)S(1)} %get-tuple-element.250, s32[]{:T(128)S(6)} %copy.48), kind=kOutput, calls=%fused_computation.3.clone.1 | convolution fusion | flops 543158272 | bytes 9715716 | tf_op jit(solution)/shard_map/while/body/eval_jaxpr/qhgd,khd->hgqk/dot_general | solution.py:83
  409.3 4.6 %fusion.39 = f32[16,256]{1,0:T(8,128)S(1)} fusion(f32[512,256,16]{1,0,2:T(8,128)} %get-tuple-element.221, f32[16,256]{1,0:T(8,128)S(1)} %bitcast.113, pred[256,512]{0,1:T(8,128)(4,1)S(1)} %broadcast_compare_fusion.2), kind=kLoop, calls=%fused_computation.5.clone.1 | loop fusion | flops 10481664 | bytes 8552448 | tf_op jit(solution)/shard_map/while/body/eval_jaxpr/reduce_sum | solution.py:91
  415.1 5.0 %bitcast_add_fusion.6 = f32[1,16,256,128]{3,2,1,0:T(8,128)} fusion(f32[1,16,256,128]{3,2,1,0:T(8,128)} %get-tuple-element.237, f32[512,256,16]{1,0,2:T(8,128)S(1)} %copy-done, f32[16,256]{1,0:T(8,128)S(1)} %bitcast.114, pred[256,512]{0,1:T(8,128)(4,1)S(1)} %broadcast_compare_fusion.2, f32[16,256]{1,0:T(8,128)S(1)} %get-tuple-element.222, ...), kind=kOutput, calls=%fused_computation.9.clone.1 | convolution fusion | flops 548929536 | bytes 12877829 | tf_op jit(solution)/shard_map/while/body/eval_jaxpr/hgqk,khd->hgqd/dot_general | solution.py:92
  420.4 4.6 %fusion.37 = (f32[16,256]{1,0:T(8,128)S(1)}, f32[512,256,16]{1,0,2:T(8,128)}) fusion(pred[256,512]{0,1:T(8,128)(4,1)S(1)} %broadcast_compare_fusion.2, bf16[256,1,16,128]{3,0,2,1:T(8,128)(2,1)S(1)} %get-tuple-element.251, bf16[16,512,1,128]{3,1,2,0:T(8,128)(2,1)S(1)} %get-tuple-element.250, s32[]{:T(128)S(6)} %copy.48), kind=kOutput, calls=%fused_computation.3.clone.1 | convolution fusion | flops 543158272 | bytes 9715716 | tf_op jit(solution)/shard_map/while/body/eval_jaxpr/qhgd,khd->hgqk/dot_general | solution.py:83
  425.0 4.6 %fusion.39 = f32[16,256]{1,0:T(8,128)S(1)} fusion(f32[512,256,16]{1,0,2:T(8,128)} %get-tuple-element.221, f32[16,256]{1,0:T(8,128)S(1)} %bitcast.113, pred[256,512]{0,1:T(8,128)(4,1)S(1)} %broadcast_compare_fusion.2), kind=kLoop, calls=%fused_computation.5.clone.1 | loop fusion | flops 10481664 | bytes 8552448 | tf_op jit(solution)/shard_map/while/body/eval_jaxpr/reduce_sum | solution.py:91
  430.8 5.0 %bitcast_add_fusion.6 = f32[1,16,256,128]{3,2,1,0:T(8,128)} fusion(f32[1,16,256,128]{3,2,1,0:T(8,128)} %get-tuple-element.237, f32[512,256,16]{1,0,2:T(8,128)S(1)} %copy-done, f32[16,256]{1,0:T(8,128)S(1)} %bitcast.114, pred[256,512]{0,1:T(8,128)(4,1)S(1)} %broadcast_compare_fusion.2, f32[16,256]{1,0:T(8,128)S(1)} %get-tuple-element.222, ...), kind=kOutput, calls=%fused_computation.9.clone.1 | convolution fusion | flops 548929536 | bytes 12877829 | tf_op jit(solution)/shard_map/while/body/eval_jaxpr/hgqk,khd->hgqd/dot_general | solution.py:92
  435.8 1.9 fusion.25
  438.4 1.2 copy.43
  (149 shorter events, 20.4 us)
Async XLA Ops:
  7.2 7.3 %copy-start.2 = (s32[64]{0:T(128)S(1)}, s32[64]{0:T(128)}, u32[]{:S(2)}) copy-start(s32[64]{0:T(128)} %param.10) | copy-start | bytes 772
  7.2 143.3 %all-gather.2.cloned.1.call-start = ((), (), s32[]{:S(2)}) async-start(), calls=%async_computation | async-start | bytes 4325376 | tf_op jit(solution)/shard_map/all_gather | solution.py:14
  152.9 1.4 copy-start.1
  190.2 5.8 %copy-start = (f32[512,256,16]{1,0,2:T(8,128)S(1)}, f32[512,256,16]{1,0,2:T(8,128)}, u32[]{:S(2)}) copy-start(f32[512,256,16]{1,0,2:T(8,128)} %get-tuple-element.221) | copy-start | bytes 25165828 | tf_op jit(solution)/shard_map/while
  205.5 5.8 %copy-start = (f32[512,256,16]{1,0,2:T(8,128)S(1)}, f32[512,256,16]{1,0,2:T(8,128)}, u32[]{:S(2)}) copy-start(f32[512,256,16]{1,0,2:T(8,128)} %get-tuple-element.221) | copy-start | bytes 25165828 | tf_op jit(solution)/shard_map/while
  221.2 5.8 %copy-start = (f32[512,256,16]{1,0,2:T(8,128)S(1)}, f32[512,256,16]{1,0,2:T(8,128)}, u32[]{:S(2)}) copy-start(f32[512,256,16]{1,0,2:T(8,128)} %get-tuple-element.221) | copy-start | bytes 25165828 | tf_op jit(solution)/shard_map/while
  236.9 5.8 %copy-start = (f32[512,256,16]{1,0,2:T(8,128)S(1)}, f32[512,256,16]{1,0,2:T(8,128)}, u32[]{:S(2)}) copy-start(f32[512,256,16]{1,0,2:T(8,128)} %get-tuple-element.221) | copy-start | bytes 25165828 | tf_op jit(solution)/shard_map/while
  252.6 5.8 %copy-start = (f32[512,256,16]{1,0,2:T(8,128)S(1)}, f32[512,256,16]{1,0,2:T(8,128)}, u32[]{:S(2)}) copy-start(f32[512,256,16]{1,0,2:T(8,128)} %get-tuple-element.221) | copy-start | bytes 25165828 | tf_op jit(solution)/shard_map/while
  268.2 5.8 %copy-start = (f32[512,256,16]{1,0,2:T(8,128)S(1)}, f32[512,256,16]{1,0,2:T(8,128)}, u32[]{:S(2)}) copy-start(f32[512,256,16]{1,0,2:T(8,128)} %get-tuple-element.221) | copy-start | bytes 25165828 | tf_op jit(solution)/shard_map/while
  283.9 5.8 %copy-start = (f32[512,256,16]{1,0,2:T(8,128)S(1)}, f32[512,256,16]{1,0,2:T(8,128)}, u32[]{:S(2)}) copy-start(f32[512,256,16]{1,0,2:T(8,128)} %get-tuple-element.221) | copy-start | bytes 25165828 | tf_op jit(solution)/shard_map/while
  299.6 5.8 %copy-start = (f32[512,256,16]{1,0,2:T(8,128)S(1)}, f32[512,256,16]{1,0,2:T(8,128)}, u32[]{:S(2)}) copy-start(f32[512,256,16]{1,0,2:T(8,128)} %get-tuple-element.221) | copy-start | bytes 25165828 | tf_op jit(solution)/shard_map/while
  315.2 5.8 %copy-start = (f32[512,256,16]{1,0,2:T(8,128)S(1)}, f32[512,256,16]{1,0,2:T(8,128)}, u32[]{:S(2)}) copy-start(f32[512,256,16]{1,0,2:T(8,128)} %get-tuple-element.221) | copy-start | bytes 25165828 | tf_op jit(solution)/shard_map/while
  330.9 5.8 %copy-start = (f32[512,256,16]{1,0,2:T(8,128)S(1)}, f32[512,256,16]{1,0,2:T(8,128)}, u32[]{:S(2)}) copy-start(f32[512,256,16]{1,0,2:T(8,128)} %get-tuple-element.221) | copy-start | bytes 25165828 | tf_op jit(solution)/shard_map/while
  346.6 5.8 %copy-start = (f32[512,256,16]{1,0,2:T(8,128)S(1)}, f32[512,256,16]{1,0,2:T(8,128)}, u32[]{:S(2)}) copy-start(f32[512,256,16]{1,0,2:T(8,128)} %get-tuple-element.221) | copy-start | bytes 25165828 | tf_op jit(solution)/shard_map/while
  362.3 5.8 %copy-start = (f32[512,256,16]{1,0,2:T(8,128)S(1)}, f32[512,256,16]{1,0,2:T(8,128)}, u32[]{:S(2)}) copy-start(f32[512,256,16]{1,0,2:T(8,128)} %get-tuple-element.221) | copy-start | bytes 25165828 | tf_op jit(solution)/shard_map/while
  377.9 5.8 %copy-start = (f32[512,256,16]{1,0,2:T(8,128)S(1)}, f32[512,256,16]{1,0,2:T(8,128)}, u32[]{:S(2)}) copy-start(f32[512,256,16]{1,0,2:T(8,128)} %get-tuple-element.221) | copy-start | bytes 25165828 | tf_op jit(solution)/shard_map/while
  393.6 5.8 %copy-start = (f32[512,256,16]{1,0,2:T(8,128)S(1)}, f32[512,256,16]{1,0,2:T(8,128)}, u32[]{:S(2)}) copy-start(f32[512,256,16]{1,0,2:T(8,128)} %get-tuple-element.221) | copy-start | bytes 25165828 | tf_op jit(solution)/shard_map/while
  409.3 5.8 %copy-start = (f32[512,256,16]{1,0,2:T(8,128)S(1)}, f32[512,256,16]{1,0,2:T(8,128)}, u32[]{:S(2)}) copy-start(f32[512,256,16]{1,0,2:T(8,128)} %get-tuple-element.221) | copy-start | bytes 25165828 | tf_op jit(solution)/shard_map/while
  424.9 5.8 %copy-start = (f32[512,256,16]{1,0,2:T(8,128)S(1)}, f32[512,256,16]{1,0,2:T(8,128)}, u32[]{:S(2)}) copy-start(f32[512,256,16]{1,0,2:T(8,128)} %get-tuple-element.221) | copy-start | bytes 25165828 | tf_op jit(solution)/shard_map/while
Sparse Core Ops, SparseCore 0:
  10.2 140.1 all-gather.1
where the time goes:
time: 447 us
  matrix products  153 us (34%)
  waiting for transfers between devices  136 us (30%)
  other arithmetic  84.4 us (19%)
  blocking collectives  29.1 us (7%)
  local copies, waits for them, and re-layouts  27.9 us (6%)
  between operations  15.5 us (3%)
    all_gather x1, waiting for transfers between devices, side_by_side(): lax.all_gather(both, axis, axis=dim, tiled=True)  136 us
    dot_general x16, matrix products, step(): jnp.einsum('hgqk,khd->hgqd', weight.astype(jnp.bfloat16), value_block, pr...  80 us
    reduce_sum x16, other arithmetic, step(): total = total * factor + jnp.sum(weight, axis=-1)  73.5 us
    dot_general x16, matrix products, step(): jnp.einsum('qhgd,khd->hgqk', query_heads, key_block, preferred_element_ty...  73.2 us
    all_gather x1, blocking collectives, on_device(): raw = lax.all_gather(local_raw, 'page', axis=1, tiled=True)  29.1 us
    while x48, local copies, waits for them, and re-layouts  19.2 us
  transfers between devices with their start and end apart: 1, of which 1 were waited for; matrix products, arithmetic and copies ran while one was open for 1% of the time, Pallas kernels for 0%

commit v1 on v0

--- a/solution.py
+++ b/solution.py
@@ -108,7 +108,9 @@
     key_pages = key_pages.reshape(slots_here, PAGE, kv_here, DH).transpose(0, 2, 1, 3)
     value_pages = value_pages.reshape(slots_here, PAGE, kv_here, DH).transpose(0, 2, 1, 3)
     local_raw = jnp.stack([key_pages, value_pages], axis=2)
-    raw = lax.all_gather(local_raw, "page", axis=1, tiled=True)
+    raw = jnp.concatenate(
+        lax.all_to_all(jnp.stack([local_raw] * lax.axis_size("page")), "page", 0, 0), axis=1
+    )
     top, total, summed = state
     result = summed / total[..., None]
     attended = jnp.transpose(result, (2, 0, 1, 3)).reshape(rows, q_here * DH).astype(jnp.bfloat16)

time: 447 us -> 460 us (1.029)
  blocking collectives: 29.1 us -> 0 us
  starting transfers between devices: 0.04 us -> 24.9 us
  matrix products: 153 us -> 168 us
    all_gather x1 -> x0, blocking collectives: 29.1 us -> none  [on_device(): raw = lax.all_gather(local_raw, 'page', axis=1, tiled=True)]
    all_to_all x0 -> x1, starting transfers between devices: none -> 24.9 us  [on_device(): lax.all_to_all(jnp.stack([local_raw] * lax.axis_size('page')), 'page', 0, 0)]
    dot_general x16, matrix products: 73.2 us -> 87.7 us  [step(): jnp.einsum('qhgd,khd->hgqk', query_heads, key_block, preferred_element_ty...]
  transfers between devices with their start and end apart: 1 -> 2, of which waited for: 1 -> 1; matrix products, arithmetic and copies ran while one was open for 1% -> 55% of each run, Pallas kernels for 0% -> 0%
where the time goes in v1:
time: 460 us; the launch traced here: 459 us
  matrix products  168 us (37%)
  waiting for transfers between devices  136 us (30%)
  other arithmetic  83.6 us (18%)
  local copies, waits for them, and re-layouts  30.3 us (7%)
  starting transfers between devices  24.9 us (5%)
  between operations  15.5 us (3%)
    all_gather x1, waiting for transfers between devices, side_by_side(): lax.all_gather(both, axis, axis=dim, tiled=True)  136 us
    dot_general x16, matrix products, step(): jnp.einsum('qhgd,khd->hgqk', query_heads, key_block, preferred_element_ty...  87.7 us
    dot_general x16, matrix products, step(): jnp.einsum('hgqk,khd->hgqd', weight.astype(jnp.bfloat16), value_block, pr...  80.2 us
    reduce_sum x16, other arithmetic, step(): total = total * factor + jnp.sum(weight, axis=-1)  73.5 us
    all_to_all x1, starting transfers between devices, on_device(): lax.all_to_all(jnp.stack([local_raw] * lax.axis_size('page')), 'page', 0, 0)  24.9 us
    while x48, local copies, waits for them, and re-layouts  19.2 us
  transfers between devices with their start and end apart: 2, of which 1 were waited for; matrix products, arithmetic and copies ran while one was open for 55% of the time, Pallas kernels for 0%

profile of v1, /device:TPU:1, one launch (start us, length us, event | category | flops | bytes accessed | tf_op | source)
XLA Modules:
  0.0 458.7 jit_solution(18090103915215577557)
XLA Ops:
  7.2 1.5 pad_maximum_fusion
  8.8 1.3 fusion.27
  12.3 1.5 copy.28
  14.8 135.6 %all-gather.2.cloned.1.call-done = bf16[8192,256]{1,0:T(8,128)(2,1)} async-done(((bf16[256,256]{1,0:T(8,128)(2,1)}), bf16[8192,256]{1,0:T(8,128)(2,1)}) %all-gather.2.cloned.1.call-update) | async-done | bytes 4194320 | tf_op jit(solution)/shard_map/all_gather | solution.py:14
  150.4 2.5 fusion.29
  152.9 1.4 copy-done.1
  155.9 24.9 %all-to-all-start = ((bf16[4,2,1,2,128,128]{5,4,3,1,2,0:T(8,128)(2,1)}), bf16[4,2,1,2,128,128]{5,4,3,1,2,0:T(8,128)(2,1)S(1)}, u32[]{:S(2)}, u32[]{:S(2)}) async-start(bf16[4,2,1,2,128,128]{5,4,3,1,2,0:T(8,128)(2,1)} %stack.38), calls=%async_computation | async-start | bytes 1048576 | tf_op jit(solution)/shard_map/all_to_all | solution.py:112
  180.8 265.2 %while.15 = (s32[]{:T(128)}, f32[1,16,256]{2,1,0:T(8,128)S(1)}, f32[1,16,256]{2,1,0:T(8,128)S(1)}, f32[1,16,256,128]{3,2,1,0:T(8,128)}, s32[16,512]{1,0:T(8,128)...) while((s32[]{:T(128)}, f32[1,16,256]{2,1,0:T(8,128)S(1)}, ...), condition=%wide.region_5.6_spmd.clone, body=%wide.region_2.5_spmd.clone.sunk | while | flops 1102733568 | bytes 65020080 | solution.py:101
  181.0 5.5 %fusion.37 = (f32[16,256]{1,0:T(8,128)S(1)}, f32[512,256,16]{1,0,2:T(8,128)}) fusion(pred[256,512]{0,1:T(8,128)(4,1)S(1)} %broadcast_compare_fusion.2, bf16[256,1,16,128]{3,0,2,1:T(8,128)(2,1)S(1)} %get-tuple-element.242, bf16[16,512,1,128]{3,1,2,0:T(8,128)(2,1)} %get-tuple-element.241, s32[]{:T(128)S(6)} %copy.48), kind=kOutput, calls=%fused_computation.3.clone.1 | convolution fusion | flops 543158272 | bytes 9715716 | tf_op jit(solution)/shard_map/while/body/eval_jaxpr/qhgd,khd->hgqk/dot_general | solution.py:83
  186.5 4.6 %fusion.39 = f32[16,256]{1,0:T(8,128)S(1)} fusion(f32[512,256,16]{1,0,2:T(8,128)} %get-tuple-element.212, f32[16,256]{1,0:T(8,128)S(1)} %bitcast.118, pred[256,512]{0,1:T(8,128)(4,1)S(1)} %broadcast_compare_fusion.2), kind=kLoop, calls=%fused_computation.5.clone.1 | loop fusion | flops 10481664 | bytes 8552448 | tf_op jit(solution)/shard_map/while/body/eval_jaxpr/reduce_sum | solution.py:91
  191.1 1.2 copy-done
  192.3 4.7 %bitcast_add_fusion.6 = f32[1,16,256,128]{3,2,1,0:T(8,128)} fusion(f32[1,16,256,128]{3,2,1,0:T(8,128)} %get-tuple-element.228, f32[512,256,16]{1,0,2:T(8,128)S(1)} %copy-done, f32[16,256]{1,0:T(8,128)S(1)} %bitcast.119, pred[256,512]{0,1:T(8,128)(4,1)S(1)} %broadcast_compare_fusion.2, f32[16,256]{1,0:T(8,128)S(1)} %get-tuple-element.213, ...), kind=kOutput, calls=%fused_computation.9.clone.1 | convolution fusion | flops 548929536 | bytes 12877829 | tf_op jit(solution)/shard_map/while/body/eval_jaxpr/hgqk,khd->hgqd/dot_general | solution.py:92
  197.3 5.5 %fusion.37 = (f32[16,256]{1,0:T(8,128)S(1)}, f32[512,256,16]{1,0,2:T(8,128)}) fusion(pred[256,512]{0,1:T(8,128)(4,1)S(1)} %broadcast_compare_fusion.2, bf16[256,1,16,128]{3,0,2,1:T(8,128)(2,1)S(1)} %get-tuple-element.242, bf16[16,512,1,128]{3,1,2,0:T(8,128)(2,1)} %get-tuple-element.241, s32[]{:T(128)S(6)} %copy.48), kind=kOutput, calls=%fused_computation.3.clone.1 | convolution fusion | flops 543158272 | bytes 9715716 | tf_op jit(solution)/shard_map/while/body/eval_jaxpr/qhgd,khd->hgqk/dot_general | solution.py:83
  202.8 4.6 %fusion.39 = f32[16,256]{1,0:T(8,128)S(1)} fusion(f32[512,256,16]{1,0,2:T(8,128)} %get-tuple-element.212, f32[16,256]{1,0:T(8,128)S(1)} %bitcast.118, pred[256,512]{0,1:T(8,128)(4,1)S(1)} %broadcast_compare_fusion.2), kind=kLoop, calls=%fused_computation.5.clone.1 | loop fusion | flops 10481664 | bytes 8552448 | tf_op jit(solution)/shard_map/while/body/eval_jaxpr/reduce_sum | solution.py:91
  207.4 1.2 copy-done
  208.6 5.0 %bitcast_add_fusion.6 = f32[1,16,256,128]{3,2,1,0:T(8,128)} fusion(f32[1,16,256,128]{3,2,1,0:T(8,128)} %get-tuple-element.228, f32[512,256,16]{1,0,2:T(8,128)S(1)} %copy-done, f32[16,256]{1,0:T(8,128)S(1)} %bitcast.119, pred[256,512]{0,1:T(8,128)(4,1)S(1)} %broadcast_compare_fusion.2, f32[16,256]{1,0:T(8,128)S(1)} %get-tuple-element.213, ...), kind=kOutput, calls=%fused_computation.9.clone.1 | convolution fusion | flops 548929536 | bytes 12877829 | tf_op jit(solution)/shard_map/while/body/eval_jaxpr/hgqk,khd->hgqd/dot_general | solution.py:92
  213.9 5.5 %fusion.37 = (f32[16,256]{1,0:T(8,128)S(1)}, f32[512,256,16]{1,0,2:T(8,128)}) fusion(pred[256,512]{0,1:T(8,128)(4,1)S(1)} %broadcast_compare_fusion.2, bf16[256,1,16,128]{3,0,2,1:T(8,128)(2,1)S(1)} %get-tuple-element.242, bf16[16,512,1,128]{3,1,2,0:T(8,128)(2,1)} %get-tuple-element.241, s32[]{:T(128)S(6)} %copy.48), kind=kOutput, calls=%fused_computation.3.clone.1 | convolution fusion | flops 543158272 | bytes 9715716 | tf_op jit(solution)/shard_map/while/body/eval_jaxpr/qhgd,khd->hgqk/dot_general | solution.py:83
  219.4 4.6 %fusion.39 = f32[16,256]{1,0:T(8,128)S(1)} fusion(f32[512,256,16]{1,0,2:T(8,128)} %get-tuple-element.212, f32[16,256]{1,0:T(8,128)S(1)} %bitcast.118, pred[256,512]{0,1:T(8,128)(4,1)S(1)} %broadcast_compare_fusion.2), kind=kLoop, calls=%fused_computation.5.clone.1 | loop fusion | flops 10481664 | bytes 8552448 | tf_op jit(solution)/shard_map/while/body/eval_jaxpr/reduce_sum | solution.py:91
  224.0 1.2 copy-done
  225.2 5.0 %bitcast_add_fusion.6 = f32[1,16,256,128]{3,2,1,0:T(8,128)} fusion(f32[1,16,256,128]{3,2,1,0:T(8,128)} %get-tuple-element.228, f32[512,256,16]{1,0,2:T(8,128)S(1)} %copy-done, f32[16,256]{1,0:T(8,128)S(1)} %bitcast.119, pred[256,512]{0,1:T(8,128)(4,1)S(1)} %broadcast_compare_fusion.2, f32[16,256]{1,0:T(8,128)S(1)} %get-tuple-element.213, ...), kind=kOutput, calls=%fused_computation.9.clone.1 | convolution fusion | flops 548929536 | bytes 12877829 | tf_op jit(solution)/shard_map/while/body/eval_jaxpr/hgqk,khd->hgqd/dot_general | solution.py:92
  230.5 5.5 %fusion.37 = (f32[16,256]{1,0:T(8,128)S(1)}, f32[512,256,16]{1,0,2:T(8,128)}) fusion(pred[256,512]{0,1:T(8,128)(4,1)S(1)} %broadcast_compare_fusion.2, bf16[256,1,16,128]{3,0,2,1:T(8,128)(2,1)S(1)} %get-tuple-element.242, bf16[16,512,1,128]{3,1,2,0:T(8,128)(2,1)} %get-tuple-element.241, s32[]{:T(128)S(6)} %copy.48), kind=kOutput, calls=%fused_computation.3.clone.1 | convolution fusion | flops 543158272 | bytes 9715716 | tf_op jit(solution)/shard_map/while/body/eval_jaxpr/qhgd,khd->hgqk/dot_general | solution.py:83
  236.0 4.6 %fusion.39 = f32[16,256]{1,0:T(8,128)S(1)} fusion(f32[512,256,16]{1,0,2:T(8,128)} %get-tuple-element.212, f32[16,256]{1,0:T(8,128)S(1)} %bitcast.118, pred[256,512]{0,1:T(8,128)(4,1)S(1)} %broadcast_compare_fusion.2), kind=kLoop, calls=%fused_computation.5.clone.1 | loop fusion | flops 10481664 | bytes 8552448 | tf_op jit(solution)/shard_map/while/body/eval_jaxpr/reduce_sum | solution.py:91
  241.8 5.0 %bitcast_add_fusion.6 = f32[1,16,256,128]{3,2,1,0:T(8,128)} fusion(f32[1,16,256,128]{3,2,1,0:T(8,128)} %get-tuple-element.228, f32[512,256,16]{1,0,2:T(8,128)S(1)} %copy-done, f32[16,256]{1,0:T(8,128)S(1)} %bitcast.119, pred[256,512]{0,1:T(8,128)(4,1)S(1)} %broadcast_compare_fusion.2, f32[16,256]{1,0:T(8,128)S(1)} %get-tuple-element.213, ...), kind=kOutput, calls=%fused_computation.9.clone.1 | convolution fusion | flops 548929536 | bytes 12877829 | tf_op jit(solution)/shard_map/while/body/eval_jaxpr/hgqk,khd->hgqd/dot_general | solution.py:92
  247.1 5.5 %fusion.37 = (f32[16,256]{1,0:T(8,128)S(1)}, f32[512,256,16]{1,0,2:T(8,128)}) fusion(pred[256,512]{0,1:T(8,128)(4,1)S(1)} %broadcast_compare_fusion.2, bf16[256,1,16,128]{3,0,2,1:T(8,128)(2,1)S(1)} %get-tuple-element.242, bf16[16,512,1,128]{3,1,2,0:T(8,128)(2,1)} %get-tuple-element.241, s32[]{:T(128)S(6)} %copy.48), kind=kOutput, calls=%fused_computation.3.clone.1 | convolution fusion | flops 543158272 | bytes 9715716 | tf_op jit(solution)/shard_map/while/body/eval_jaxpr/qhgd,khd->hgqk/dot_general | solution.py:83
  252.6 4.6 %fusion.39 = f32[16,256]{1,0:T(8,128)S(1)} fusion(f32[512,256,16]{1,0,2:T(8,128)} %get-tuple-element.212, f32[16,256]{1,0:T(8,128)S(1)} %bitcast.118, pred[256,512]{0,1:T(8,128)(4,1)S(1)} %broadcast_compare_fusion.2), kind=kLoop, calls=%fused_computation.5.clone.1 | loop fusion | flops 10481664 | bytes 8552448 | tf_op jit(solution)/shard_map/while/body/eval_jaxpr/reduce_sum | solution.py:91
  258.4 5.0 %bitcast_add_fusion.6 = f32[1,16,256,128]{3,2,1,0:T(8,128)} fusion(f32[1,16,256,128]{3,2,1,0:T(8,128)} %get-tuple-element.228, f32[512,256,16]{1,0,2:T(8,128)S(1)} %copy-done, f32[16,256]{1,0:T(8,128)S(1)} %bitcast.119, pred[256,512]{0,1:T(8,128)(4,1)S(1)} %broadcast_compare_fusion.2, f32[16,256]{1,0:T(8,128)S(1)} %get-tuple-element.213, ...), kind=kOutput, calls=%fused_computation.9.clone.1 | convolution fusion | flops 548929536 | bytes 12877829 | tf_op jit(solution)/shard_map/while/body/eval_jaxpr/hgqk,khd->hgqd/dot_general | solution.py:92
  263.7 5.5 %fusion.37 = (f32[16,256]{1,0:T(8,128)S(1)}, f32[512,256,16]{1,0,2:T(8,128)}) fusion(pred[256,512]{0,1:T(8,128)(4,1)S(1)} %broadcast_compare_fusion.2, bf16[256,1,16,128]{3,0,2,1:T(8,128)(2,1)S(1)} %get-tuple-element.242, bf16[16,512,1,128]{3,1,2,0:T(8,128)(2,1)} %get-tuple-element.241, s32[]{:T(128)S(6)} %copy.48), kind=kOutput, calls=%fused_computation.3.clone.1 | convolution fusion | flops 543158272 | bytes 9715716 | tf_op jit(solution)/shard_map/while/body/eval_jaxpr/qhgd,khd->hgqk/dot_general | solution.py:83
  269.2 4.6 %fusion.39 = f32[16,256]{1,0:T(8,128)S(1)} fusion(f32[512,256,16]{1,0,2:T(8,128)} %get-tuple-element.212, f32[16,256]{1,0:T(8,128)S(1)} %bitcast.118, pred[256,512]{0,1:T(8,128)(4,1)S(1)} %broadcast_compare_fusion.2), kind=kLoop, calls=%fused_computation.5.clone.1 | loop fusion | flops 10481664 | bytes 8552448 | tf_op jit(solution)/shard_map/while/body/eval_jaxpr/reduce_sum | solution.py:91
  273.8 1.2 copy-done
  275.0 5.0 %bitcast_add_fusion.6 = f32[1,16,256,128]{3,2,1,0:T(8,128)} fusion(f32[1,16,256,128]{3,2,1,0:T(8,128)} %get-tuple-element.228, f32[512,256,16]{1,0,2:T(8,128)S(1)} %copy-done, f32[16,256]{1,0:T(8,128)S(1)} %bitcast.119, pred[256,512]{0,1:T(8,128)(4,1)S(1)} %broadcast_compare_fusion.2, f32[16,256]{1,0:T(8,128)S(1)} %get-tuple-element.213, ...), kind=kOutput, calls=%fused_computation.9.clone.1 | convolution fusion | flops 548929536 | bytes 12877829 | tf_op jit(solution)/shard_map/while/body/eval_jaxpr/hgqk,khd->hgqd/dot_general | solution.py:92
  280.3 5.5 %fusion.37 = (f32[16,256]{1,0:T(8,128)S(1)}, f32[512,256,16]{1,0,2:T(8,128)}) fusion(pred[256,512]{0,1:T(8,128)(4,1)S(1)} %broadcast_compare_fusion.2, bf16[256,1,16,128]{3,0,2,1:T(8,128)(2,1)S(1)} %get-tuple-element.242, bf16[16,512,1,128]{3,1,2,0:T(8,128)(2,1)} %get-tuple-element.241, s32[]{:T(128)S(6)} %copy.48), kind=kOutput, calls=%fused_computation.3.clone.1 | convolution fusion | flops 543158272 | bytes 9715716 | tf_op jit(solution)/shard_map/while/body/eval_jaxpr/qhgd,khd->hgqk/dot_general | solution.py:83
  285.8 4.6 %fusion.39 = f32[16,256]{1,0:T(8,128)S(1)} fusion(f32[512,256,16]{1,0,2:T(8,128)} %get-tuple-element.212, f32[16,256]{1,0:T(8,128)S(1)} %bitcast.118, pred[256,512]{0,1:T(8,128)(4,1)S(1)} %broadcast_compare_fusion.2), kind=kLoop, calls=%fused_computation.5.clone.1 | loop fusion | flops 10481664 | bytes 8552448 | tf_op jit(solution)/shard_map/while/body/eval_jaxpr/reduce_sum | solution.py:91
  291.6 5.0 %bitcast_add_fusion.6 = f32[1,16,256,128]{3,2,1,0:T(8,128)} fusion(f32[1,16,256,128]{3,2,1,0:T(8,128)} %get-tuple-element.228, f32[512,256,16]{1,0,2:T(8,128)S(1)} %copy-done, f32[16,256]{1,0:T(8,128)S(1)} %bitcast.119, pred[256,512]{0,1:T(8,128)(4,1)S(1)} %broadcast_compare_fusion.2, f32[16,256]{1,0:T(8,128)S(1)} %get-tuple-element.213, ...), kind=kOutput, calls=%fused_computation.9.clone.1 | convolution fusion | flops 548929536 | bytes 12877829 | tf_op jit(solution)/shard_map/while/body/eval_jaxpr/hgqk,khd->hgqd/dot_general | solution.py:92
  296.9 5.5 %fusion.37 = (f32[16,256]{1,0:T(8,128)S(1)}, f32[512,256,16]{1,0,2:T(8,128)}) fusion(pred[256,512]{0,1:T(8,128)(4,1)S(1)} %broadcast_compare_fusion.2, bf16[256,1,16,128]{3,0,2,1:T(8,128)(2,1)S(1)} %get-tuple-element.242, bf16[16,512,1,128]{3,1,2,0:T(8,128)(2,1)} %get-tuple-element.241, s32[]{:T(128)S(6)} %copy.48), kind=kOutput, calls=%fused_computation.3.clone.1 | convolution fusion | flops 543158272 | bytes 9715716 | tf_op jit(solution)/shard_map/while/body/eval_jaxpr/qhgd,khd->hgqk/dot_general | solution.py:83
  302.4 4.6 %fusion.39 = f32[16,256]{1,0:T(8,128)S(1)} fusion(f32[512,256,16]{1,0,2:T(8,128)} %get-tuple-element.212, f32[16,256]{1,0:T(8,128)S(1)} %bitcast.118, pred[256,512]{0,1:T(8,128)(4,1)S(1)} %broadcast_compare_fusion.2), kind=kLoop, calls=%fused_computation.5.clone.1 | loop fusion | flops 10481664 | bytes 8552448 | tf_op jit(solution)/shard_map/while/body/eval_jaxpr/reduce_sum | solution.py:91
  308.2 5.0 %bitcast_add_fusion.6 = f32[1,16,256,128]{3,2,1,0:T(8,128)} fusion(f32[1,16,256,128]{3,2,1,0:T(8,128)} %get-tuple-element.228, f32[512,256,16]{1,0,2:T(8,128)S(1)} %copy-done, f32[16,256]{1,0:T(8,128)S(1)} %bitcast.119, pred[256,512]{0,1:T(8,128)(4,1)S(1)} %broadcast_compare_fusion.2, f32[16,256]{1,0:T(8,128)S(1)} %get-tuple-element.213, ...), kind=kOutput, calls=%fused_computation.9.clone.1 | convolution fusion | flops 548929536 | bytes 12877829 | tf_op jit(solution)/shard_map/while/body/eval_jaxpr/hgqk,khd->hgqd/dot_general | solution.py:92
  313.5 5.5 %fusion.37 = (f32[16,256]{1,0:T(8,128)S(1)}, f32[512,256,16]{1,0,2:T(8,128)}) fusion(pred[256,512]{0,1:T(8,128)(4,1)S(1)} %broadcast_compare_fusion.2, bf16[256,1,16,128]{3,0,2,1:T(8,128)(2,1)S(1)} %get-tuple-element.242, bf16[16,512,1,128]{3,1,2,0:T(8,128)(2,1)} %get-tuple-element.241, s32[]{:T(128)S(6)} %copy.48), kind=kOutput, calls=%fused_computation.3.clone.1 | convolution fusion | flops 543158272 | bytes 9715716 | tf_op jit(solution)/shard_map/while/body/eval_jaxpr/qhgd,khd->hgqk/dot_general | solution.py:83
  319.0 4.6 %fusion.39 = f32[16,256]{1,0:T(8,128)S(1)} fusion(f32[512,256,16]{1,0,2:T(8,128)} %get-tuple-element.212, f32[16,256]{1,0:T(8,128)S(1)} %bitcast.118, pred[256,512]{0,1:T(8,128)(4,1)S(1)} %broadcast_compare_fusion.2), kind=kLoop, calls=%fused_computation.5.clone.1 | loop fusion | flops 10481664 | bytes 8552448 | tf_op jit(solution)/shard_map/while/body/eval_jaxpr/reduce_sum | solution.py:91
  324.8 5.0 %bitcast_add_fusion.6 = f32[1,16,256,128]{3,2,1,0:T(8,128)} fusion(f32[1,16,256,128]{3,2,1,0:T(8,128)} %get-tuple-element.228, f32[512,256,16]{1,0,2:T(8,128)S(1)} %copy-done, f32[16,256]{1,0:T(8,128)S(1)} %bitcast.119, pred[256,512]{0,1:T(8,128)(4,1)S(1)} %broadcast_compare_fusion.2, f32[16,256]{1,0:T(8,128)S(1)} %get-tuple-element.213, ...), kind=kOutput, calls=%fused_computation.9.clone.1 | convolution fusion | flops 548929536 | bytes 12877829 | tf_op jit(solution)/shard_map/while/body/eval_jaxpr/hgqk,khd->hgqd/dot_general | solution.py:92
  330.0 5.5 %fusion.37 = (f32[16,256]{1,0:T(8,128)S(1)}, f32[512,256,16]{1,0,2:T(8,128)}) fusion(pred[256,512]{0,1:T(8,128)(4,1)S(1)} %broadcast_compare_fusion.2, bf16[256,1,16,128]{3,0,2,1:T(8,128)(2,1)S(1)} %get-tuple-element.242, bf16[16,512,1,128]{3,1,2,0:T(8,128)(2,1)} %get-tuple-element.241, s32[]{:T(128)S(6)} %copy.48), kind=kOutput, calls=%fused_computation.3.clone.1 | convolution fusion | flops 543158272 | bytes 9715716 | tf_op jit(solution)/shard_map/while/body/eval_jaxpr/qhgd,khd->hgqk/dot_general | solution.py:83
  335.6 4.6 %fusion.39 = f32[16,256]{1,0:T(8,128)S(1)} fusion(f32[512,256,16]{1,0,2:T(8,128)} %get-tuple-element.212, f32[16,256]{1,0:T(8,128)S(1)} %bitcast.118, pred[256,512]{0,1:T(8,128)(4,1)S(1)} %broadcast_compare_fusion.2), kind=kLoop, calls=%fused_computation.5.clone.1 | loop fusion | flops 10481664 | bytes 8552448 | tf_op jit(solution)/shard_map/while/body/eval_jaxpr/reduce_sum | solution.py:91
  340.2 1.2 copy-done
  341.4 5.0 %bitcast_add_fusion.6 = f32[1,16,256,128]{3,2,1,0:T(8,128)} fusion(f32[1,16,256,128]{3,2,1,0:T(8,128)} %get-tuple-element.228, f32[512,256,16]{1,0,2:T(8,128)S(1)} %copy-done, f32[16,256]{1,0:T(8,128)S(1)} %bitcast.119, pred[256,512]{0,1:T(8,128)(4,1)S(1)} %broadcast_compare_fusion.2, f32[16,256]{1,0:T(8,128)S(1)} %get-tuple-element.213, ...), kind=kOutput, calls=%fused_computation.9.clone.1 | convolution fusion | flops 548929536 | bytes 12877829 | tf_op jit(solution)/shard_map/while/body/eval_jaxpr/hgqk,khd->hgqd/dot_general | solution.py:92
  346.6 5.5 %fusion.37 = (f32[16,256]{1,0:T(8,128)S(1)}, f32[512,256,16]{1,0,2:T(8,128)}) fusion(pred[256,512]{0,1:T(8,128)(4,1)S(1)} %broadcast_compare_fusion.2, bf16[256,1,16,128]{3,0,2,1:T(8,128)(2,1)S(1)} %get-tuple-element.242, bf16[16,512,1,128]{3,1,2,0:T(8,128)(2,1)} %get-tuple-element.241, s32[]{:T(128)S(6)} %copy.48), kind=kOutput, calls=%fused_computation.3.clone.1 | convolution fusion | flops 543158272 | bytes 9715716 | tf_op jit(solution)/shard_map/while/body/eval_jaxpr/qhgd,khd->hgqk/dot_general | solution.py:83
  352.2 4.6 %fusion.39 = f32[16,256]{1,0:T(8,128)S(1)} fusion(f32[512,256,16]{1,0,2:T(8,128)} %get-tuple-element.212, f32[16,256]{1,0:T(8,128)S(1)} %bitcast.118, pred[256,512]{0,1:T(8,128)(4,1)S(1)} %broadcast_compare_fusion.2), kind=kLoop, calls=%fused_computation.5.clone.1 | loop fusion | flops 10481664 | bytes 8552448 | tf_op jit(solution)/shard_map/while/body/eval_jaxpr/reduce_sum | solution.py:91
  358.0 5.0 %bitcast_add_fusion.6 = f32[1,16,256,128]{3,2,1,0:T(8,128)} fusion(f32[1,16,256,128]{3,2,1,0:T(8,128)} %get-tuple-element.228, f32[512,256,16]{1,0,2:T(8,128)S(1)} %copy-done, f32[16,256]{1,0:T(8,128)S(1)} %bitcast.119, pred[256,512]{0,1:T(8,128)(4,1)S(1)} %broadcast_compare_fusion.2, f32[16,256]{1,0:T(8,128)S(1)} %get-tuple-element.213, ...), kind=kOutput, calls=%fused_computation.9.clone.1 | convolution fusion | flops 548929536 | bytes 12877829 | tf_op jit(solution)/shard_map/while/body/eval_jaxpr/hgqk,khd->hgqd/dot_general | solution.py:92
  363.2 5.5 %fusion.37 = (f32[16,256]{1,0:T(8,128)S(1)}, f32[512,256,16]{1,0,2:T(8,128)}) fusion(pred[256,512]{0,1:T(8,128)(4,1)S(1)} %broadcast_compare_fusion.2, bf16[256,1,16,128]{3,0,2,1:T(8,128)(2,1)S(1)} %get-tuple-element.242, bf16[16,512,1,128]{3,1,2,0:T(8,128)(2,1)} %get-tuple-element.241, s32[]{:T(128)S(6)} %copy.48), kind=kOutput, calls=%fused_computation.3.clone.1 | convolution fusion | flops 543158272 | bytes 9715716 | tf_op jit(solution)/shard_map/while/body/eval_jaxpr/qhgd,khd->hgqk/dot_general | solution.py:83
  368.8 4.6 %fusion.39 = f32[16,256]{1,0:T(8,128)S(1)} fusion(f32[512,256,16]{1,0,2:T(8,128)} %get-tuple-element.212, f32[16,256]{1,0:T(8,128)S(1)} %bitcast.118, pred[256,512]{0,1:T(8,128)(4,1)S(1)} %broadcast_compare_fusion.2), kind=kLoop, calls=%fused_computation.5.clone.1 | loop fusion | flops 10481664 | bytes 8552448 | tf_op jit(solution)/shard_map/while/body/eval_jaxpr/reduce_sum | solution.py:91
  374.6 5.0 %bitcast_add_fusion.6 = f32[1,16,256,128]{3,2,1,0:T(8,128)} fusion(f32[1,16,256,128]{3,2,1,0:T(8,128)} %get-tuple-element.228, f32[512,256,16]{1,0,2:T(8,128)S(1)} %copy-done, f32[16,256]{1,0:T(8,128)S(1)} %bitcast.119, pred[256,512]{0,1:T(8,128)(4,1)S(1)} %broadcast_compare_fusion.2, f32[16,256]{1,0:T(8,128)S(1)} %get-tuple-element.213, ...), kind=kOutput, calls=%fused_computation.9.clone.1 | convolution fusion | flops 548929536 | bytes 12877829 | tf_op jit(solution)/shard_map/while/body/eval_jaxpr/hgqk,khd->hgqd/dot_general | solution.py:92
  379.8 5.5 %fusion.37 = (f32[16,256]{1,0:T(8,128)S(1)}, f32[512,256,16]{1,0,2:T(8,128)}) fusion(pred[256,512]{0,1:T(8,128)(4,1)S(1)} %broadcast_compare_fusion.2, bf16[256,1,16,128]{3,0,2,1:T(8,128)(2,1)S(1)} %get-tuple-element.242, bf16[16,512,1,128]{3,1,2,0:T(8,128)(2,1)} %get-tuple-element.241, s32[]{:T(128)S(6)} %copy.48), kind=kOutput, calls=%fused_computation.3.clone.1 | convolution fusion | flops 543158272 | bytes 9715716 | tf_op jit(solution)/shard_map/while/body/eval_jaxpr/qhgd,khd->hgqk/dot_general | solution.py:83
  385.4 4.6 %fusion.39 = f32[16,256]{1,0:T(8,128)S(1)} fusion(f32[512,256,16]{1,0,2:T(8,128)} %get-tuple-element.212, f32[16,256]{1,0:T(8,128)S(1)} %bitcast.118, pred[256,512]{0,1:T(8,128)(4,1)S(1)} %broadcast_compare_fusion.2), kind=kLoop, calls=%fused_computation.5.clone.1 | loop fusion | flops 10481664 | bytes 8552448 | tf_op jit(solution)/shard_map/while/body/eval_jaxpr/reduce_sum | solution.py:91
  391.2 5.0 %bitcast_add_fusion.6 = f32[1,16,256,128]{3,2,1,0:T(8,128)} fusion(f32[1,16,256,128]{3,2,1,0:T(8,128)} %get-tuple-element.228, f32[512,256,16]{1,0,2:T(8,128)S(1)} %copy-done, f32[16,256]{1,0:T(8,128)S(1)} %bitcast.119, pred[256,512]{0,1:T(8,128)(4,1)S(1)} %broadcast_compare_fusion.2, f32[16,256]{1,0:T(8,128)S(1)} %get-tuple-element.213, ...), kind=kOutput, calls=%fused_computation.9.clone.1 | convolution fusion | flops 548929536 | bytes 12877829 | tf_op jit(solution)/shard_map/while/body/eval_jaxpr/hgqk,khd->hgqd/dot_general | solution.py:92
  396.4 5.5 %fusion.37 = (f32[16,256]{1,0:T(8,128)S(1)}, f32[512,256,16]{1,0,2:T(8,128)}) fusion(pred[256,512]{0,1:T(8,128)(4,1)S(1)} %broadcast_compare_fusion.2, bf16[256,1,16,128]{3,0,2,1:T(8,128)(2,1)S(1)} %get-tuple-element.242, bf16[16,512,1,128]{3,1,2,0:T(8,128)(2,1)} %get-tuple-element.241, s32[]{:T(128)S(6)} %copy.48), kind=kOutput, calls=%fused_computation.3.clone.1 | convolution fusion | flops 543158272 | bytes 9715716 | tf_op jit(solution)/shard_map/while/body/eval_jaxpr/qhgd,khd->hgqk/dot_general | solution.py:83
  401.9 4.6 %fusion.39 = f32[16,256]{1,0:T(8,128)S(1)} fusion(f32[512,256,16]{1,0,2:T(8,128)} %get-tuple-element.212, f32[16,256]{1,0:T(8,128)S(1)} %bitcast.118, pred[256,512]{0,1:T(8,128)(4,1)S(1)} %broadcast_compare_fusion.2), kind=kLoop, calls=%fused_computation.5.clone.1 | loop fusion | flops 10481664 | bytes 8552448 | tf_op jit(solution)/shard_map/while/body/eval_jaxpr/reduce_sum | solution.py:91
  406.6 1.2 copy-done
  407.8 5.0 %bitcast_add_fusion.6 = f32[1,16,256,128]{3,2,1,0:T(8,128)} fusion(f32[1,16,256,128]{3,2,1,0:T(8,128)} %get-tuple-element.228, f32[512,256,16]{1,0,2:T(8,128)S(1)} %copy-done, f32[16,256]{1,0:T(8,128)S(1)} %bitcast.119, pred[256,512]{0,1:T(8,128)(4,1)S(1)} %broadcast_compare_fusion.2, f32[16,256]{1,0:T(8,128)S(1)} %get-tuple-element.213, ...), kind=kOutput, calls=%fused_computation.9.clone.1 | convolution fusion | flops 548929536 | bytes 12877829 | tf_op jit(solution)/shard_map/while/body/eval_jaxpr/hgqk,khd->hgqd/dot_general | solution.py:92
  413.0 5.5 %fusion.37 = (f32[16,256]{1,0:T(8,128)S(1)}, f32[512,256,16]{1,0,2:T(8,128)}) fusion(pred[256,512]{0,1:T(8,128)(4,1)S(1)} %broadcast_compare_fusion.2, bf16[256,1,16,128]{3,0,2,1:T(8,128)(2,1)S(1)} %get-tuple-element.242, bf16[16,512,1,128]{3,1,2,0:T(8,128)(2,1)} %get-tuple-element.241, s32[]{:T(128)S(6)} %copy.48), kind=kOutput, calls=%fused_computation.3.clone.1 | convolution fusion | flops 543158272 | bytes 9715716 | tf_op jit(solution)/shard_map/while/body/eval_jaxpr/qhgd,khd->hgqk/dot_general | solution.py:83
  418.5 4.6 %fusion.39 = f32[16,256]{1,0:T(8,128)S(1)} fusion(f32[512,256,16]{1,0,2:T(8,128)} %get-tuple-element.212, f32[16,256]{1,0:T(8,128)S(1)} %bitcast.118, pred[256,512]{0,1:T(8,128)(4,1)S(1)} %broadcast_compare_fusion.2), kind=kLoop, calls=%fused_computation.5.clone.1 | loop fusion | flops 10481664 | bytes 8552448 | tf_op jit(solution)/shard_map/while/body/eval_jaxpr/reduce_sum | solution.py:91
  424.4 5.0 %bitcast_add_fusion.6 = f32[1,16,256,128]{3,2,1,0:T(8,128)} fusion(f32[1,16,256,128]{3,2,1,0:T(8,128)} %get-tuple-element.228, f32[512,256,16]{1,0,2:T(8,128)S(1)} %copy-done, f32[16,256]{1,0:T(8,128)S(1)} %bitcast.119, pred[256,512]{0,1:T(8,128)(4,1)S(1)} %broadcast_compare_fusion.2, f32[16,256]{1,0:T(8,128)S(1)} %get-tuple-element.213, ...), kind=kOutput, calls=%fused_computation.9.clone.1 | convolution fusion | flops 548929536 | bytes 12877829 | tf_op jit(solution)/shard_map/while/body/eval_jaxpr/hgqk,khd->hgqd/dot_general | solution.py:92
  429.6 5.5 %fusion.37 = (f32[16,256]{1,0:T(8,128)S(1)}, f32[512,256,16]{1,0,2:T(8,128)}) fusion(pred[256,512]{0,1:T(8,128)(4,1)S(1)} %broadcast_compare_fusion.2, bf16[256,1,16,128]{3,0,2,1:T(8,128)(2,1)S(1)} %get-tuple-element.242, bf16[16,512,1,128]{3,1,2,0:T(8,128)(2,1)} %get-tuple-element.241, s32[]{:T(128)S(6)} %copy.48), kind=kOutput, calls=%fused_computation.3.clone.1 | convolution fusion | flops 543158272 | bytes 9715716 | tf_op jit(solution)/shard_map/while/body/eval_jaxpr/qhgd,khd->hgqk/dot_general | solution.py:83
  435.1 4.6 %fusion.39 = f32[16,256]{1,0:T(8,128)S(1)} fusion(f32[512,256,16]{1,0,2:T(8,128)} %get-tuple-element.212, f32[16,256]{1,0:T(8,128)S(1)} %bitcast.118, pred[256,512]{0,1:T(8,128)(4,1)S(1)} %broadcast_compare_fusion.2), kind=kLoop, calls=%fused_computation.5.clone.1 | loop fusion | flops 10481664 | bytes 8552448 | tf_op jit(solution)/shard_map/while/body/eval_jaxpr/reduce_sum | solution.py:91
  441.0 5.0 %bitcast_add_fusion.6 = f32[1,16,256,128]{3,2,1,0:T(8,128)} fusion(f32[1,16,256,128]{3,2,1,0:T(8,128)} %get-tuple-element.228, f32[512,256,16]{1,0,2:T(8,128)S(1)} %copy-done, f32[16,256]{1,0:T(8,128)S(1)} %bitcast.119, pred[256,512]{0,1:T(8,128)(4,1)S(1)} %broadcast_compare_fusion.2, f32[16,256]{1,0:T(8,128)S(1)} %get-tuple-element.213, ...), kind=kOutput, calls=%fused_computation.9.clone.1 | convolution fusion | flops 548929536 | bytes 12877829 | tf_op jit(solution)/shard_map/while/body/eval_jaxpr/hgqk,khd->hgqd/dot_general | solution.py:92
  446.0 1.9 fusion.25
  448.6 1.2 copy.43
  (156 shorter events, 21.9 us)
Async XLA Ops:
  7.2 7.3 %copy-start.3 = (s32[64]{0:T(128)S(1)}, s32[64]{0:T(128)}, u32[]{:S(2)}) copy-start(s32[64]{0:T(128)} %param.10) | copy-start | bytes 772
  7.2 143.3 %all-gather.2.cloned.1.call-start = ((), (), s32[]{:S(2)}) async-start(), calls=%async_computation.1 | async-start | bytes 4325376 | tf_op jit(solution)/shard_map/all_gather | solution.py:14
  152.9 1.4 copy-start.1
  152.9 2.0 copy-start.2
  155.9 294.0 %all-to-all-start = ((bf16[4,2,1,2,128,128]{5,4,3,1,2,0:T(8,128)(2,1)}), bf16[4,2,1,2,128,128]{5,4,3,1,2,0:T(8,128)(2,1)S(1)}, u32[]{:S(2)}, u32[]{:S(2)}) async-start(bf16[4,2,1,2,128,128]{5,4,3,1,2,0:T(8,128)(2,1)} %stack.38), calls=%async_computation | async-start | bytes 1048576 | tf_op jit(solution)/shard_map/all_to_all | solution.py:112
  186.5 5.8 %copy-start = (f32[512,256,16]{1,0,2:T(8,128)S(1)}, f32[512,256,16]{1,0,2:T(8,128)}, u32[]{:S(2)}) copy-start(f32[512,256,16]{1,0,2:T(8,128)} %get-tuple-element.212) | copy-start | bytes 25165828 | tf_op jit(solution)/shard_map/while
  202.8 5.8 %copy-start = (f32[512,256,16]{1,0,2:T(8,128)S(1)}, f32[512,256,16]{1,0,2:T(8,128)}, u32[]{:S(2)}) copy-start(f32[512,256,16]{1,0,2:T(8,128)} %get-tuple-element.212) | copy-start | bytes 25165828 | tf_op jit(solution)/shard_map/while
  219.4 5.8 %copy-start = (f32[512,256,16]{1,0,2:T(8,128)S(1)}, f32[512,256,16]{1,0,2:T(8,128)}, u32[]{:S(2)}) copy-start(f32[512,256,16]{1,0,2:T(8,128)} %get-tuple-element.212) | copy-start | bytes 25165828 | tf_op jit(solution)/shard_map/while
  236.0 5.8 %copy-start = (f32[512,256,16]{1,0,2:T(8,128)S(1)}, f32[512,256,16]{1,0,2:T(8,128)}, u32[]{:S(2)}) copy-start(f32[512,256,16]{1,0,2:T(8,128)} %get-tuple-element.212) | copy-start | bytes 25165828 | tf_op jit(solution)/shard_map/while
  252.6 5.8 %copy-start = (f32[512,256,16]{1,0,2:T(8,128)S(1)}, f32[512,256,16]{1,0,2:T(8,128)}, u32[]{:S(2)}) copy-start(f32[512,256,16]{1,0,2:T(8,128)} %get-tuple-element.212) | copy-start | bytes 25165828 | tf_op jit(solution)/shard_map/while
  269.2 5.8 %copy-start = (f32[512,256,16]{1,0,2:T(8,128)S(1)}, f32[512,256,16]{1,0,2:T(8,128)}, u32[]{:S(2)}) copy-start(f32[512,256,16]{1,0,2:T(8,128)} %get-tuple-element.212) | copy-start | bytes 25165828 | tf_op jit(solution)/shard_map/while
  285.8 5.8 %copy-start = (f32[512,256,16]{1,0,2:T(8,128)S(1)}, f32[512,256,16]{1,0,2:T(8,128)}, u32[]{:S(2)}) copy-start(f32[512,256,16]{1,0,2:T(8,128)} %get-tuple-element.212) | copy-start | bytes 25165828 | tf_op jit(solution)/shard_map/while
  302.4 5.8 %copy-start = (f32[512,256,16]{1,0,2:T(8,128)S(1)}, f32[512,256,16]{1,0,2:T(8,128)}, u32[]{:S(2)}) copy-start(f32[512,256,16]{1,0,2:T(8,128)} %get-tuple-element.212) | copy-start | bytes 25165828 | tf_op jit(solution)/shard_map/while
  318.9 5.8 %copy-start = (f32[512,256,16]{1,0,2:T(8,128)S(1)}, f32[512,256,16]{1,0,2:T(8,128)}, u32[]{:S(2)}) copy-start(f32[512,256,16]{1,0,2:T(8,128)} %get-tuple-element.212) | copy-start | bytes 25165828 | tf_op jit(solution)/shard_map/while
  335.5 5.8 %copy-start = (f32[512,256,16]{1,0,2:T(8,128)S(1)}, f32[512,256,16]{1,0,2:T(8,128)}, u32[]{:S(2)}) copy-start(f32[512,256,16]{1,0,2:T(8,128)} %get-tuple-element.212) | copy-start | bytes 25165828 | tf_op jit(solution)/shard_map/while
  352.1 5.8 %copy-start = (f32[512,256,16]{1,0,2:T(8,128)S(1)}, f32[512,256,16]{1,0,2:T(8,128)}, u32[]{:S(2)}) copy-start(f32[512,256,16]{1,0,2:T(8,128)} %get-tuple-element.212) | copy-start | bytes 25165828 | tf_op jit(solution)/shard_map/while
  368.7 5.8 %copy-start = (f32[512,256,16]{1,0,2:T(8,128)S(1)}, f32[512,256,16]{1,0,2:T(8,128)}, u32[]{:S(2)}) copy-start(f32[512,256,16]{1,0,2:T(8,128)} %get-tuple-element.212) | copy-start | bytes 25165828 | tf_op jit(solution)/shard_map/while
  385.3 5.8 %copy-start = (f32[512,256,16]{1,0,2:T(8,128)S(1)}, f32[512,256,16]{1,0,2:T(8,128)}, u32[]{:S(2)}) copy-start(f32[512,256,16]{1,0,2:T(8,128)} %get-tuple-element.212) | copy-start | bytes 25165828 | tf_op jit(solution)/shard_map/while
  401.9 5.8 %copy-start = (f32[512,256,16]{1,0,2:T(8,128)S(1)}, f32[512,256,16]{1,0,2:T(8,128)}, u32[]{:S(2)}) copy-start(f32[512,256,16]{1,0,2:T(8,128)} %get-tuple-element.212) | copy-start | bytes 25165828 | tf_op jit(solution)/shard_map/while
  418.5 5.8 %copy-start = (f32[512,256,16]{1,0,2:T(8,128)S(1)}, f32[512,256,16]{1,0,2:T(8,128)}, u32[]{:S(2)}) copy-start(f32[512,256,16]{1,0,2:T(8,128)} %get-tuple-element.212) | copy-start | bytes 25165828 | tf_op jit(solution)/shard_map/while
  435.1 5.8 %copy-start = (f32[512,256,16]{1,0,2:T(8,128)S(1)}, f32[512,256,16]{1,0,2:T(8,128)}, u32[]{:S(2)}) copy-start(f32[512,256,16]{1,0,2:T(8,128)} %get-tuple-element.212) | copy-start | bytes 25165828 | tf_op jit(solution)/shard_map/while
Sparse Core Ops, SparseCore 0:
  10.2 140.1 all-gather.1
